TPU v7x, 512 devices: a whole 4x8x8 slice. The times are simulated.
512 devices in a mesh: wide: 128 (over y, z, core), narrow: 4 (over x).
Axes of the slice: x: 4, y: 8, z: 8, core: 2. Of those that a mesh axis runs over, the one named last changes fastest.
Arguments:
- grad_out: bfloat16 [32768, 512], P('wide', 'narrow'), may hold values from -24 to 24
- relu_mask: int32 [32768, 512], P('wide', 'narrow'), may hold values 0 or 1
- features: bfloat16 [32768, 512], P('wide', 'narrow'), may hold values from -6 to 6
- hop1_mean: bfloat16 [32768, 512], P('wide', 'narrow'), may hold values from -6 to 6
- hop2_mean: bfloat16 [32768, 512], P('wide', 'narrow'), may hold values from -6 to 6
- w_self: bfloat16 [512, 512], P('narrow'), may hold values from -0.25 to 0.25
- w_hop1: bfloat16 [512, 512], P('narrow'), may hold values from -0.25 to 0.25
- w_hop2: bfloat16 [512, 512], P('narrow'), may hold values from -0.25 to 0.25
- norm: float32 [32768], P('wide'), may hold values from 0.05 to 1
- tile_src: int32 [16384], P('wide'), may hold values from 0 to 1
- tile_owner: int32 [16384], P('wide'), may hold values from 0 to 127, as said below
- tile_block: int32 [16384], P('wide'), may hold values from 0 to 1
- tile_cols: int32 [16384, 128, 8], P('wide'), may hold values from 0 to 127
Outputs:
- grad_features: bfloat16 [32768, 512], P('wide', 'narrow')
- weight_grads: float32 [3, 512, 512], P(None, 'wide', 'narrow')
Inputs may be any that keep to these rules, and one draw needn't show every extreme that they name: `tile_owner`: the 128 tiles of one device name every device once as owner.
All inputs are finite; a program needn't handle non-finite values. No bound on the sum of `relu_mask` on one device may be relied on, other than what follows from the above.
Results may differ from a plain program's by a relative error of at most 0.0054.
Values may be sent and summed in bfloat16 or wider, within the bound.
No kernel may reach another device: no remote copies, remote signals or barrier semaphores. Data moves between devices by JAX's collectives and lax.ppermute only.
A program may use at most 64 MiB of HBM per device.

v0:
```python
import jax
import jax.numpy as jnp
from jax import lax
from jax.sharding import PartitionSpec as P


def tile_pattern(tile_cols):
    positions = jnp.arange(tile_cols.shape[1], dtype=jnp.int32)
    summed = jnp.zeros(tile_cols.shape[:2] + (tile_cols.shape[1],), jnp.int32)
    for column in range(tile_cols.shape[2]):
        summed = summed + (tile_cols[:, :, column, None] == positions).astype(jnp.int32)
    return summed.astype(jnp.bfloat16)


def on_device(
    grad_out,
    relu_mask,
    features,
    hop1_mean,
    hop2_mean,
    w_self,
    w_hop1,
    w_hop2,
    norm,
    tile_src,
    tile_owner,
    tile_block,
    tile_cols,
):
    node_count = features.shape[0]
    local_width = features.shape[1]
    block_rows = tile_cols.shape[1]
    row_blocks = node_count // block_rows
    owner_count = lax.axis_size("wide")
    gated = grad_out * relu_mask.astype(jnp.bfloat16)
    gated_full = lax.all_gather(gated, "narrow", axis=1, tiled=True)
    row_scale = norm[:, None]
    slot_ids = jnp.full((owner_count, 1), -1.0, jnp.float32)
    slot_ids = slot_ids.at[tile_owner, 0].set(tile_block.astype(jnp.float32)).astype(jnp.bfloat16)
    block_marks = jnp.arange(row_blocks, dtype=jnp.float32).astype(jnp.bfloat16)

    def combine_arrived(arrived, arrived_ids):
        select = (arrived_ids[:, 0][None, :] == block_marks[:, None]).astype(jnp.bfloat16)
        summed = jnp.einsum("bs,sjd->bjd", select, arrived, preferred_element_type=jnp.float32)
        return summed.reshape(node_count, local_width)

    pattern = tile_pattern(tile_cols)

    def transpose_hop(scaled):
        picked = scaled.reshape(row_blocks, block_rows, local_width)[tile_src]
        products = jnp.einsum(
            "trj,trd->tjd", pattern, picked, preferred_element_type=jnp.float32
        ).astype(jnp.bfloat16)
        outgoing = (
            jnp.zeros((owner_count, block_rows, local_width), jnp.bfloat16)
            .at[tile_owner]
            .set(products)
        )
        arrived, arrived_ids = (
            lax.all_to_all(outgoing, "wide", split_axis=0, concat_axis=0, tiled=True),
            lax.all_to_all(slot_ids, "wide", split_axis=0, concat_axis=0, tiled=True),
        )
        return combine_arrived(arrived, arrived_ids)

    def project(weight):
        return lax.dot_general(
            gated_full, weight, (((1,), (1,)), ((), ())), preferred_element_type=jnp.float32
        )

    scaled2 = (row_scale * project(w_hop2)).astype(jnp.bfloat16)
    agg2 = transpose_hop(scaled2)
    scaled1 = (row_scale * (project(w_hop1) + agg2)).astype(jnp.bfloat16)
    agg1 = transpose_hop(scaled1)
    grad_features = (project(w_self) + agg1).astype(jnp.bfloat16)
    partial_grads = jnp.stack(
        [
            jnp.einsum("ro,rd->od", gated_full, operand, preferred_element_type=jnp.float32)
            for operand in (features, hop1_mean, hop2_mean)
        ]
    )
    weight_grads = lax.psum_scatter(partial_grads, "wide", scatter_dimension=1, tiled=True)
    return (grad_features, weight_grads)


def solution(mesh):
    placed = (
        P("wide", "narrow"),
        P("wide", "narrow"),
        P("wide", "narrow"),
        P("wide", "narrow"),
        P("wide", "narrow"),
        P("narrow", None),
        P("narrow", None),
        P("narrow", None),
        P("wide"),
        P("wide"),
        P("wide"),
        P("wide"),
        P("wide", None, None),
    )
    return jax.shard_map(
        on_device,
        mesh=mesh,
        in_specs=placed,
        out_specs=(P("wide", "narrow"), P(None, "wide", "narrow")),
        check_vma=False,
    )
```

profile of v0, /device:TPU:1, one launch (start us, length us, event | category | flops | bytes accessed | tf_op | source)
XLA Modules:
  0.0 537.8 jit_solution(16396398977169809282)
XLA Ops:
  8.5 1.0 scatter_custom_fusion
  10.3 18.4 %all-to-all-start = ((bf16[128,1,1]{2,1,0:T(2,128)(2,1)}), bf16[128,1,1]{2,1,0:T(2,128)(2,1)S(1)}, u32[]{:S(2)}, u32[]{:S(2)}) async-start(bf16[128,1,1]{2,1,0:T(2,128)(2,1)} %copy.26), calls=%async_computation | async-start | bytes 131072 | tf_op jit(solution)/shard_map/all_to_all | solution.py:61
  28.7 3.4 fusion.18
  32.1 1.0 convert_multiply_fusion
  33.1 10.5 %all_gather.3 = bf16[256,512]{1,0:T(8,128)(2,1)S(1)} all-gather(bf16[256,128]{1,0:T(8,128)(2,1)S(1)} %convert_multiply_fusion), channel_id=1, replica_groups=mesh['wide'=128,'narrow'=4] {'narrow'}, dimensions={1}, use_global_device_ids=true | all-gather | bytes 327680 | tf_op jit(solution)/shard_map/all_gather | solution.py:36
  44.2 0.9 fusion.7
  45.1 3.1 gather_fusion
  48.2 12.0 %convolution_convert_fusion.1 = bf16[128,128,128]{2,1,0:T(8,128)(2,1)} fusion(bf16[128,128,128]{2,1,0:T(8,128)(2,1)} %gather_fusion, s32[128,128]{1,0:T(8,128)S(1)} %bitcast.58, s32[128,128]{1,0:T(8,128)S(1)} %bitcast.60, s32[128,128]{1,0:T(8,128)S(1)} %bitcast.48, s32[128,128]{1,0:T(8,128)S(1)} %bitcast.50, s32[128,128]{1,0:T(8,128)S(1)} %bitcast.52, ...), kind=kOutput, calls=%fused_computation.19 | convolution fusion | flops 589299712 | bytes 8912896 | tf_op jit(solution)/shard_map/trj,trd->tjd/dot_general | solution.py:51
  60.2 3.0 broadcast.17.clone
  63.2 19.4 %scatter_fusion = bf16[128,128,128]{2,1,0:T(8,128)(2,1)} fusion(bf16[128,128,128]{2,1,0:T(8,128)(2,1)} %broadcast.17.clone, s32[128]{0:T(128)S(1)} %compare_select_fusion.1, bf16[128,128,128]{2,1,0:T(8,128)(2,1)} %convolution_convert_fusion.1), kind=kCustom, calls=%fused_computation.3 | custom fusion | bytes 12583424 | tf_op jit(solution)/shard_map/scatter | solution.py:57
  82.6 15.6 %all-to-all-start.1 = ((bf16[128,128,128]{2,1,0:T(8,128)(2,1)}), bf16[128,128,128]{2,1,0:T(8,128)(2,1)}, u32[]{:S(2)}, u32[]{:S(2)}) async-start(bf16[128,128,128]{2,1,0:T(8,128)(2,1)} %scatter_fusion), calls=%async_computation.1 | async-start | bytes 8388608 | tf_op jit(solution)/shard_map/all_to_all | solution.py:60
  98.3 1.0 reduce
  99.3 94.6 %all-to-all-done.1 = bf16[128,128,128]{2,1,0:T(8,128)(2,1)} async-done(((bf16[128,128,128]{2,1,0:T(8,128)(2,1)}), bf16[128,128,128]{2,1,0:T(8,128)(2,1)}, u32[]{:S(2)}, u32[]{:S(2)}) %all-to-all-start.1) | async-done | bytes 4194336 | tf_op jit(solution)/shard_map/all_to_all | solution.py:60
  193.9 4.5 fusion.2
  198.7 3.1 gather_fusion.1
  201.8 12.0 %convolution_convert_fusion = bf16[128,128,128]{2,1,0:T(8,128)(2,1)} fusion(bf16[128,128,128]{2,1,0:T(8,128)(2,1)} %gather_fusion.1, s32[128,128]{1,0:T(8,128)S(1)} %bitcast.59, s32[128,128]{1,0:T(8,128)S(1)} %bitcast.61, s32[128,128]{1,0:T(8,128)S(1)} %bitcast.49, s32[128,128]{1,0:T(8,128)S(1)} %bitcast.51, s32[128,128]{1,0:T(8,128)S(1)} %bitcast.53, ...), kind=kOutput, calls=%fused_computation.18 | convolution fusion | flops 589299712 | bytes 8912896 | tf_op jit(solution)/shard_map/trj,trd->tjd/dot_general | solution.py:51
  213.8 3.0 broadcast.17
  216.8 19.4 %scatter_fusion.1 = bf16[128,128,128]{2,1,0:T(8,128)(2,1)} fusion(bf16[128,128,128]{2,1,0:T(8,128)(2,1)} %broadcast.17, s32[128]{0:T(128)S(1)} %compare_select_fusion.1, bf16[128,128,128]{2,1,0:T(8,128)(2,1)} %convolution_convert_fusion), kind=kCustom, calls=%fused_computation.4 | custom fusion | bytes 12583424 | tf_op jit(solution)/shard_map/scatter | solution.py:57
  236.2 16.7 %all-to-all-start.2 = ((bf16[128,128,128]{2,1,0:T(8,128)(2,1)}), bf16[128,128,128]{2,1,0:T(8,128)(2,1)}, u32[]{:S(2)}, u32[]{:S(2)}) async-start(bf16[128,128,128]{2,1,0:T(8,128)(2,1)} %scatter_fusion.1), calls=%async_computation.2 | async-start | bytes 8388608 | tf_op jit(solution)/shard_map/all_to_all | solution.py:60
  254.0 0.9 pad_maximum_fusion
  255.0 1.3 dynamic-slice
  256.9 267.3 %all-reduce.4.cloned.1.call-done = f32[3,512,128]{2,1,0:T(8,128)} async-done(((f32[3,512,128]{2,1,0:T(8,128)}), f32[3,512,128]{2,1,0:T(8,128)}) %all-reduce.4.cloned.1.call-update) | async-done | bytes 786448
  524.2 1.3 constant_dynamic-slice_fusion
  525.5 4.5 fusion
  (32 shorter events, 5.0 us)
Async XLA Ops:
  7.2 37.1 %copy-start = (bf16[128,512]{1,0:T(8,128)(2,1)S(1)}, bf16[128,512]{1,0:T(8,128)(2,1)}, u32[]{:S(2)}) copy-start(bf16[128,512]{1,0:T(8,128)(2,1)} %param.20) | copy-start | bytes 393220
  10.3 72.3 %all-to-all-start = ((bf16[128,1,1]{2,1,0:T(2,128)(2,1)}), bf16[128,1,1]{2,1,0:T(2,128)(2,1)S(1)}, u32[]{:S(2)}, u32[]{:S(2)}) async-start(bf16[128,1,1]{2,1,0:T(2,128)(2,1)} %copy.26), calls=%async_computation | async-start | bytes 131072 | tf_op jit(solution)/shard_map/all_to_all | solution.py:61
  82.6 111.3 %all-to-all-start.1 = ((bf16[128,128,128]{2,1,0:T(8,128)(2,1)}), bf16[128,128,128]{2,1,0:T(8,128)(2,1)}, u32[]{:S(2)}, u32[]{:S(2)}) async-start(bf16[128,128,128]{2,1,0:T(8,128)(2,1)} %scatter_fusion), calls=%async_computation.1 | async-start | bytes 8388608 | tf_op jit(solution)/shard_map/all_to_all | solution.py:60
  98.2 100.2 %copy-start.1 = (bf16[128,512]{1,0:T(8,128)(2,1)S(1)}, bf16[128,512]{1,0:T(8,128)(2,1)}, u32[]{:S(2)}) copy-start(bf16[128,512]{1,0:T(8,128)(2,1)} %param.19) | copy-start | bytes 393220
  98.3 100.2 %copy-start.6 = (f32[256]{0:T(256)S(1)}, f32[256]{0:T(256)}, u32[]{:S(2)}) copy-start(f32[256]{0:T(256)} %param.21) | copy-start | bytes 3076
  236.2 17.0 %copy-start.3 = (bf16[256,128]{1,0:T(8,128)(2,1)S(1)}, bf16[256,128]{1,0:T(8,128)(2,1)}, u32[]{:S(2)}) copy-start(bf16[256,128]{1,0:T(8,128)(2,1)} %param.17) | copy-start | bytes 196612
  236.2 17.3 %copy-start.4 = (bf16[256,128]{1,0:T(8,128)(2,1)S(1)}, bf16[256,128]{1,0:T(8,128)(2,1)}, u32[]{:S(2)}) copy-start(bf16[256,128]{1,0:T(8,128)(2,1)} %param.16) | copy-start | bytes 196612
  236.2 17.5 %copy-start.5 = (bf16[256,128]{1,0:T(8,128)(2,1)S(1)}, bf16[256,128]{1,0:T(8,128)(2,1)}, u32[]{:S(2)}) copy-start(bf16[256,128]{1,0:T(8,128)(2,1)} %param.15) | copy-start | bytes 196612
  236.2 289.3 %all-to-all-start.2 = ((bf16[128,128,128]{2,1,0:T(8,128)(2,1)}), bf16[128,128,128]{2,1,0:T(8,128)(2,1)}, u32[]{:S(2)}, u32[]{:S(2)}) async-start(bf16[128,128,128]{2,1,0:T(8,128)(2,1)} %scatter_fusion.1), calls=%async_computation.2 | async-start | bytes 8388608 | tf_op jit(solution)/shard_map/all_to_all | solution.py:60
  252.9 271.3 %all-reduce.4.cloned.1.call-start = ((), (), s32[]{:S(2)}) async-start(), calls=%async_computation.3 | async-start | bytes 1572864
  253.5 276.6 %copy-start.2 = (bf16[128,512]{1,0:T(8,128)(2,1)S(1)}, bf16[128,512]{1,0:T(8,128)(2,1)}, u32[]{:S(2)}) copy-start(bf16[128,512]{1,0:T(8,128)(2,1)} %param.18) | copy-start | bytes 393220
Sparse Core Ops, SparseCore 0:
  256.9 267.2 all-reduce.3
where the time goes:
time: 540 us; the launch traced here: 538 us
  waiting for transfers between devices  362 us (67%)
  local copies, waits for them, and re-layouts  58.7 us (11%)
  starting transfers between devices  51 us (9%)
  matrix products  35.8 us (7%)
  between operations  14.9 us (3%)
  blocking collectives  10.5 us (2%)
    unnamed x2, waiting for transfers between devices  267 us
    all_to_all x2, waiting for transfers between devices, transpose_hop(): lax.all_to_all(outgoing, 'wide', split_axis=0, concat_axis=0, tiled=True)  94.6 us
    scatter x2, local copies, waits for them, and re-layouts, transpose_hop(): outgoing = jnp.zeros((owner_count, block_rows, local_width), jnp.bfloat16...  38.8 us
    all_to_all x2, starting transfers between devices, transpose_hop(): lax.all_to_all(outgoing, 'wide', split_axis=0, concat_axis=0, tiled=True)  32.3 us
    dot_general x2, matrix products, transpose_hop(): jnp.einsum('trj,trd->tjd', pattern, picked, preferred_element_type=jnp.fl...  24 us
    all_to_all x1, starting transfers between devices, transpose_hop(): lax.all_to_all(slot_ids, 'wide', split_axis=0, concat_axis=0, tiled=True)  18.4 us
  transfers between devices with their start and end apart: 4, of which 2 were waited for; matrix products, arithmetic and copies ran while one was open for 9% of the time, Pallas kernels for 0%

commit v1 on v0

v1 whole, which is shorter than its diff:
```python
import jax
import jax.numpy as jnp
from jax import lax
from jax.experimental import pallas as pl
from jax.experimental.pallas import tpu as pltpu
from jax.sharding import PartitionSpec as P

ROWS = 128
NNZ = 8
GROUP = 16


def route_kernel(owner_ref, src_ref, block_ref, cols_ref, out_ref):
    row = lax.broadcasted_iota(jnp.int32, (NNZ, ROWS), 0)

    def step(t, carry):
        cols = cols_ref[t]
        marks = jnp.where(row == 0, src_ref[t], jnp.where(row == 1, block_ref[t], 0))
        both = jnp.concatenate([cols, marks], axis=0).astype(jnp.float32)
        out_ref[owner_ref[t]] = both.astype(jnp.bfloat16)
        return carry

    lax.fori_loop(0, cols_ref.shape[0], step, 0)


def route(tile_owner, tile_src, tile_block, cols):
    tiles = cols.shape[0]
    return pl.pallas_call(
        route_kernel,
        out_shape=jax.ShapeDtypeStruct((tiles, 2 * NNZ, ROWS), jnp.bfloat16),
        grid_spec=pltpu.PrefetchScalarGridSpec(
            num_scalar_prefetch=3,
            grid=(1,),
            in_specs=[pl.BlockSpec(cols.shape, lambda i, *_: (0, 0, 0))],
            out_specs=pl.BlockSpec((tiles, 2 * NNZ, ROWS), lambda i, *_: (0, 0, 0)),
        ),
        cost_estimate=pl.CostEstimate(flops=1 << 20, bytes_accessed=1 << 20, transcendentals=0),
    )(tile_owner, tile_src, tile_block, cols)


def pattern_kernel(block_ref, cols_ref, out_ref):
    first = pl.program_id(0) * GROUP
    position = lax.broadcasted_iota(jnp.int32, (ROWS, ROWS), 0).astype(jnp.float32).astype(jnp.bfloat16)
    one = jnp.ones((ROWS, ROWS), jnp.bfloat16)
    zero = jnp.zeros((ROWS, ROWS), jnp.bfloat16)
    for d in range(GROUP):
        cols = cols_ref[d].astype(jnp.float32)
        count = zero
        for k in range(NNZ):
            line = jnp.broadcast_to(cols[k : k + 1, :], (ROWS, ROWS)).astype(jnp.bfloat16)
            count = count + jnp.where(line == position, one, zero)
        low = block_ref[first + d] == 0
        lanes = pl.ds(d * ROWS, ROWS)
        out_ref[0:ROWS, lanes] = jnp.where(low, count, zero)
        out_ref[ROWS : 2 * ROWS, lanes] = jnp.where(low, zero, count)


def build_pattern(block, arrived):
    tiles = arrived.shape[0]
    return pl.pallas_call(
        pattern_kernel,
        out_shape=jax.ShapeDtypeStruct((2 * ROWS, tiles * ROWS), jnp.bfloat16),
        grid_spec=pltpu.PrefetchScalarGridSpec(
            num_scalar_prefetch=1,
            grid=(tiles // GROUP,),
            in_specs=[pl.BlockSpec((GROUP, 2 * NNZ, ROWS), lambda i, *_: (i, 0, 0))],
            out_specs=pl.BlockSpec((2 * ROWS, GROUP * ROWS), lambda i, *_: (0, i)),
        ),
        cost_estimate=pl.CostEstimate(flops=1 << 26, bytes_accessed=9 << 20, transcendentals=0),
    )(block, arrived)


def hop_kernel(src_ref, rows_ref, pattern_ref, own_ref, scale_ref, out_ref, total_ref):
    step = pl.program_id(0)
    picked = []
    for d in range(GROUP):
        start = pl.multiple_of(d * 2 * ROWS + src_ref[step * GROUP + d] * ROWS, ROWS)
        picked.append(rows_ref[pl.ds(start, ROWS), :])
    part = jnp.dot(
        pattern_ref[...], jnp.concatenate(picked, axis=0), preferred_element_type=jnp.float32
    )

    @pl.when(step == 0)
    def _():
        total_ref[...] = own_ref[...] + part

    @pl.when(step > 0)
    def _():
        total_ref[...] += part

    @pl.when(step == pl.num_programs(0) - 1)
    def _():
        out_ref[...] = (scale_ref[...] * total_ref[...]).astype(jnp.bfloat16)


def hop(src, rows, pattern, own, scale):
    nodes, width = own.shape
    steps = rows.shape[0] // (GROUP * nodes)
    return pl.pallas_call(
        hop_kernel,
        out_shape=jax.ShapeDtypeStruct((nodes, width), jnp.bfloat16),
        grid_spec=pltpu.PrefetchScalarGridSpec(
            num_scalar_prefetch=1,
            grid=(steps,),
            in_specs=[
                pl.BlockSpec((GROUP * nodes, width), lambda i, *_: (i, 0)),
                pl.BlockSpec((nodes, GROUP * ROWS), lambda i, *_: (0, i)),
                pl.BlockSpec((nodes, width), lambda i, *_: (0, 0)),
                pl.BlockSpec((nodes, 1), lambda i, *_: (0, 0)),
            ],
            out_specs=pl.BlockSpec((nodes, width), lambda i, *_: (0, 0)),
            scratch_shapes=[pltpu.VMEM((nodes, width), jnp.float32)],
        ),
        cost_estimate=pl.CostEstimate(flops=1 << 30, bytes_accessed=17 << 20, transcendentals=0),
    )(src, rows, pattern, own, scale)


def on_device(
    grad_out,
    relu_mask,
    features,
    hop1_mean,
    hop2_mean,
    w_self,
    w_hop1,
    w_hop2,
    norm,
    tile_src,
    tile_owner,
    tile_block,
    tile_cols,
):
    gated = grad_out * relu_mask.astype(jnp.bfloat16)
    gated_full = lax.all_gather(gated, "narrow", axis=1, tiled=True)
    row_scale = norm[:, None]

    def project(weight):
        return lax.dot_general(
            gated_full, weight, (((1,), (1,)), ((), ())), preferred_element_type=jnp.float32
        )

    outgoing = route(tile_owner, tile_src, tile_block, jnp.swapaxes(tile_cols, 1, 2))
    scaled2 = (row_scale * project(w_hop2)).astype(jnp.bfloat16)
    scaled2, outgoing = lax.optimization_barrier((scaled2, outgoing))
    rows2 = lax.all_gather(scaled2, "wide", axis=0, tiled=True)
    arrived = lax.all_to_all(outgoing, "wide", split_axis=0, concat_axis=0, tiled=True)
    source = arrived[:, NNZ, 0].astype(jnp.int32)
    block = arrived[:, NNZ + 1, 0].astype(jnp.int32)
    pattern = build_pattern(block, arrived)
    scaled1 = hop(source, rows2, pattern, project(w_hop1), row_scale)
    partial_grads = jnp.stack(
        [
            jnp.einsum("ro,rd->od", gated_full, operand, preferred_element_type=jnp.float32)
            for operand in (features, hop1_mean, hop2_mean)
        ]
    )
    scaled1, partial_grads = lax.optimization_barrier((scaled1, partial_grads))
    rows1 = lax.all_gather(scaled1, "wide", axis=0, tiled=True)
    count = lax.axis_size("wide")
    kinds, outs, width = partial_grads.shape
    spread = lax.all_to_all(
        partial_grads.reshape(kinds, count, outs // count, width),
        "wide",
        split_axis=1,
        concat_axis=1,
        tiled=True,
    )
    weight_grads = spread.sum(axis=1)
    grad_features = hop(source, rows1, pattern, project(w_self), jnp.ones_like(row_scale))
    return (grad_features, weight_grads)


def solution(mesh):
    placed = (
        P("wide", "narrow"),
        P("wide", "narrow"),
        P("wide", "narrow"),
        P("wide", "narrow"),
        P("wide", "narrow"),
        P("narrow", None),
        P("narrow", None),
        P("narrow", None),
        P("wide"),
        P("wide"),
        P("wide"),
        P("wide"),
        P("wide", None, None),
    )
    return jax.shard_map(
        on_device,
        mesh=mesh,
        in_specs=placed,
        out_specs=(P("wide", "narrow"), P(None, "wide", "narrow")),
        check_vma=False,
    )
```

time: 540 us -> 244 us (0.45)
  waiting for transfers between devices: 362 us -> 138 us
  local copies, waits for them, and re-layouts: 58.7 us -> 3.18 us
  Pallas kernels: 0 us -> 33.5 us
  matrix products: 35.8 us -> 7.48 us
  starting transfers between devices: 51 us -> 29.2 us
    unnamed x2, waiting for transfers between devices: 267 us -> 0.03 us
    all_gather x0 -> x2, waiting for transfers between devices: none -> 98.7 us  [the longest x1 54.7 us: on_device(): rows1 = lax.all_gather(scaled1, 'wide', axis=0, tiled=True)]
    all_to_all x3 -> x2, waiting for transfers between devices: 94.6 us -> 39.3 us  [the longest x1 25.5 us: on_device(): lax.all_to_all(partial_grads.reshape(kinds, count, outs // count, width),...]
    scatter x3 -> x0, local copies, waits for them, and re-layouts: 39.7 us -> none  [the longest x2 38.8 us: transpose_hop(): outgoing = jnp.zeros((owner_count, block_rows, local_width), jnp.bfloat16...]
    pallas_call x0 -> x4, Pallas kernels: none -> 33.5 us  [the longest x2 21.3 us: hop(): pl.pallas_call(hop_kernel, out_shape=jax.ShapeDtypeStruct((nodes, width),...]
    dot_general x4 -> x0, matrix products: 33 us -> none  [the longest x2 24 us: transpose_hop(): jnp.einsum('trj,trd->tjd', pattern, picked, preferred_element_type=jnp.fl...]
    all_to_all x3 -> x2, starting transfers between devices: 50.7 us -> 29.1 us  [the longest x1 20.1 us: on_device(): lax.all_to_all(outgoing, 'wide', split_axis=0, concat_axis=0, tiled=True)]
    gather x2 -> x0, local copies, waits for them, and re-layouts: 6.12 us -> none  [transpose_hop(): picked = scaled.reshape(row_blocks, block_rows, local_width)[tile_src]]
  transfers between devices with their start and end apart: 4 -> 4, of which waited for: 2 -> 4; matrix products, arithmetic and copies ran while one was open for 9% -> 6% of each run, Pallas kernels for 0% -> 4%
where the time goes in v1:
time: 244 us; the launch traced here: 243 us
  waiting for transfers between devices  138 us (57%)
  Pallas kernels  33.5 us (14%)
  starting transfers between devices  29.2 us (12%)
  between operations  14.1 us (6%)
  blocking collectives  10.3 us (4%)
  matrix products  7.48 us (3%)
  other arithmetic  7.02 us (3%)
  local copies, waits for them, and re-layouts  3.18 us (1%)
    all_gather x1, waiting for transfers between devices, on_device(): rows1 = lax.all_gather(scaled1, 'wide', axis=0, tiled=True)  54.7 us
    all_gather x1, waiting for transfers between devices, on_device(): rows2 = lax.all_gather(scaled2, 'wide', axis=0, tiled=True)  44 us
    all_to_all x1, waiting for transfers between devices, on_device(): lax.all_to_all(partial_grads.reshape(kinds, count, outs // count, width),...  25.5 us
    pallas_call x2, Pallas kernels, hop(): pl.pallas_call(hop_kernel, out_shape=jax.ShapeDtypeStruct((nodes, width),...  21.3 us
    all_to_all x1, starting transfers between devices, on_device(): lax.all_to_all(outgoing, 'wide', split_axis=0, concat_axis=0, tiled=True)  20.1 us
    all_to_all x1, waiting for transfers between devices, on_device(): lax.all_to_all(outgoing, 'wide', split_axis=0, concat_axis=0, tiled=True)  13.8 us
    all_gather x1, blocking collectives, on_device(): gated_full = lax.all_gather(gated, 'narrow', axis=1, tiled=True)  10.3 us
    all_to_all x1, starting transfers between devices, on_device(): lax.all_to_all(partial_grads.reshape(kinds, count, outs // count, width),...  8.99 us
  transfers between devices with their start and end apart: 4, of which 4 were waited for; matrix products, arithmetic and copies ran while one was open for 6% of the time, Pallas kernels for 4%

profile of v1, /device:TPU:1, one launch (start us, length us, event | category | flops | bytes accessed | tf_op | source)
XLA Modules:
  0.0 242.8 jit_solution(9666713302698978855)
XLA Ops:
  7.2 1.0 convert_multiply_fusion
  8.2 10.3 %all_gather.9 = bf16[256,512]{1,0:T(8,128)(2,1)S(1)} all-gather(bf16[256,128]{1,0:T(8,128)(2,1)S(1)} %convert_multiply_fusion), channel_id=1, replica_groups=mesh['wide'=128,'narrow'=4] {'narrow'}, dimensions={1}, use_global_device_ids=true | all-gather | bytes 327680 | tf_op jit(solution)/shard_map/all_gather | solution.py:134
  18.5 1.5 fusion
  20.1 3.6 %shard_map.140 = bf16[128,16,128]{2,1,0:T(8,128)(2,1)} custom-call(s32[128]{0:T(128)} %owner_ref.1, s32[128]{0:T(128)} %src_ref.1, s32[128]{0:T(128)} %block_ref.1, s32[128,8,128]{2,1,0:T(8,128)} %bitcast.22), custom_call_target="tpu_custom_call" | custom-call | flops 1048576 | bytes 1048576 | tf_op jit(solution)/shard_map/pallas_call | solution.py:28
  23.7 20.1 %all-to-all-start = ((bf16[128,16,128]{2,1,0:T(8,128)(2,1)}), bf16[128,16,128]{2,1,0:T(8,128)(2,1)S(1)}, u32[]{:S(2)}, u32[]{:S(2)}) async-start(bf16[128,16,128]{2,1,0:T(8,128)(2,1)} %shard_map.140), calls=%async_computation | async-start | bytes 1048576 | tf_op jit(solution)/shard_map/all_to_all | solution.py:146
  43.8 1.5 copy.16.scale_ref
  45.3 1.1 convolution_bitcast_fusion
  46.4 1.1 convolution_bitcast_fusion.1
  47.5 1.1 convolution_bitcast_fusion.2
  48.6 0.1 pad_maximum_fusion
  48.7 1.8 fusion.3.own_ref
  50.4 13.8 %all-to-all-done.cols_ref = bf16[128,16,128]{2,1,0:T(8,128)(2,1)S(1)} async-done(((bf16[128,16,128]{2,1,0:T(8,128)(2,1)}), bf16[128,16,128]{2,1,0:T(8,128)(2,1)S(1)}, u32[]{:S(2)}, u32[]{:S(2)}) %all-to-all-start) | async-done | bytes 524320 | tf_op jit(solution)/shard_map/all_to_all | solution.py:146
  64.2 5.2 %fusion.1 = (s32[128]{0:T(128)}, s32[128]{0:T(128)}) fusion(bf16[128,16,128]{2,1,0:T(8,128)(2,1)S(1)} %all-to-all-done.cols_ref), kind=kLoop, calls=%fused_computation.7 | loop fusion | flops 256 | bytes 1536 | tf_op jit(solution)/shard_map/convert_element_type | solution.py:148
  69.4 8.7 %shard_map.141.pattern_ref = bf16[256,16384]{1,0:T(8,128)(2,1)} custom-call(s32[128]{0:T(128)} %get-tuple-element.10.block_ref, bf16[128,16,128]{2,1,0:T(8,128)(2,1)} %copy-done.1), custom_call_target="tpu_custom_call" | custom-call | flops 67108864 | bytes 9437184 | tf_op jit(solution)/shard_map/pallas_call | solution.py:60
  78.1 44.0 %all-gather.3.cloned.1.call-done.rows_ref = bf16[32768,128]{1,0:T(8,128)(2,1)} async-done(((bf16[256,128]{1,0:T(8,128)(2,1)}), bf16[32768,128]{1,0:T(8,128)(2,1)}) %all-gather.3.cloned.1.call-update) | async-done | bytes 8388624 | tf_op jit(solution)/shard_map/all_gather | solution.py:145
  122.1 10.7 %shard_map.142 = bf16[256,128]{1,0:T(8,128)(2,1)} custom-call(s32[128]{0:T(128)} %get-tuple-element.11.src_ref, bf16[32768,128]{1,0:T(8,128)(2,1)} %all-gather.3.cloned.1.call-done.rows_ref, bf16[256,16384]{1,0:T(8,128)(2,1)} %shard_map.141.pattern_ref, f32[256,128]{1,0:T(8,128)} %fusion.3.own_ref, f32[256,1]{1,0:T(8,128)} %copy.16.scale_ref), custom_call_target="tpu_custom_call" | custom-call | flops 1073741824 | bytes 17825792 | tf_op jit(solution)/shard_map/pallas_call | solution.py:99
  132.8 1.0 copy.17
  133.9 9.0 %all-to-all-start.1 = ((f32[3,128,4,128]{3,2,0,1:T(4,128)}), f32[3,128,4,128]{3,2,0,1:T(4,128)S(1)}, u32[]{:S(2)}, u32[]{:S(2)}) async-start(f32[3,128,4,128]{3,2,0,1:T(4,128)} %copy.17), calls=%async_computation.1 | async-start | bytes 1572864 | tf_op jit(solution)/shard_map/all_to_all | solution.py:161
  142.9 0.9 fusion.4.own_ref
  143.8 25.5 %all-to-all-done.1 = f32[3,128,4,128]{3,2,0,1:T(4,128)S(1)} async-done(((f32[3,128,4,128]{3,2,0,1:T(4,128)}), f32[3,128,4,128]{3,2,0,1:T(4,128)S(1)}, u32[]{:S(2)}, u32[]{:S(2)}) %all-to-all-start.1) | async-done | bytes 786464 | tf_op jit(solution)/shard_map/all_to_all | solution.py:161
  169.3 0.8 reduce_sum.9
  170.1 54.7 %all-gather.5.cloned.1.call-done.rows_ref = bf16[32768,128]{1,0:T(8,128)(2,1)} async-done(((bf16[256,128]{1,0:T(8,128)(2,1)}), bf16[32768,128]{1,0:T(8,128)(2,1)}) %all-gather.5.cloned.1.call-update) | async-done | bytes 8388624 | tf_op jit(solution)/shard_map/all_gather | solution.py:158
  224.8 0.7 broadcast_in_dim.7.scale_ref
  225.4 10.6 %shard_map.143 = bf16[256,128]{1,0:T(8,128)(2,1)} custom-call(s32[128]{0:T(128)} %get-tuple-element.11.src_ref, bf16[32768,128]{1,0:T(8,128)(2,1)} %all-gather.5.cloned.1.call-done.rows_ref, bf16[256,16384]{1,0:T(8,128)(2,1)} %shard_map.141.pattern_ref, f32[256,128]{1,0:T(8,128)} %fusion.4.own_ref, f32[256,1]{1,0:T(8,128)} %broadcast_in_dim.7.scale_ref), custom_call_target="tpu_custom_call" | custom-call | flops 1073741824 | bytes 17825792 | tf_op jit(solution)/shard_map/pallas_call | solution.py:99
  (10 shorter events, 0.1 us)
Async XLA Ops:
  7.2 11.4 %copy-start = (bf16[128,512]{1,0:T(8,128)(2,1)S(1)}, bf16[128,512]{1,0:T(8,128)(2,1)}, u32[]{:S(2)}) copy-start(bf16[128,512]{1,0:T(8,128)(2,1)} %param.20) | copy-start | bytes 393220
  7.2 114.9 %all-gather.3.cloned.1.call-start = ((), (), s32[]{:S(2)}) async-start(), calls=%async_computation.2 | async-start | bytes 8454144 | tf_op jit(solution)/shard_map/all_gather | solution.py:145
  23.7 40.5 %all-to-all-start = ((bf16[128,16,128]{2,1,0:T(8,128)(2,1)}), bf16[128,16,128]{2,1,0:T(8,128)(2,1)S(1)}, u32[]{:S(2)}, u32[]{:S(2)}) async-start(bf16[128,16,128]{2,1,0:T(8,128)(2,1)} %shard_map.140), calls=%async_computation | async-start | bytes 1048576 | tf_op jit(solution)/shard_map/all_to_all | solution.py:146
  43.8 181.0 %all-gather.5.cloned.1.call-start = ((), (), s32[]{:S(2)}) async-start(), calls=%async_computation.3 | async-start | bytes 8454144 | tf_op jit(solution)/shard_map/all_gather | solution.py:158
  64.2 5.2 %copy-start.1 = (bf16[128,16,128]{2,1,0:T(8,128)(2,1)}, bf16[128,16,128]{2,1,0:T(8,128)(2,1)S(1)}, u32[]{:S(2)}) copy-start(bf16[128,16,128]{2,1,0:T(8,128)(2,1)S(1)} %all-to-all-done.cols_ref) | copy-start | bytes 1572868
  122.1 20.8 %copy-start.2 = (bf16[128,512]{1,0:T(8,128)(2,1)S(1)}, bf16[128,512]{1,0:T(8,128)(2,1)}, u32[]{:S(2)}) copy-start(bf16[128,512]{1,0:T(8,128)(2,1)} %param.18) | copy-start | bytes 393220
  133.9 35.4 %all-to-all-start.1 = ((f32[3,128,4,128]{3,2,0,1:T(4,128)}), f32[3,128,4,128]{3,2,0,1:T(4,128)S(1)}, u32[]{:S(2)}, u32[]{:S(2)}) async-start(f32[3,128,4,128]{3,2,0,1:T(4,128)} %copy.17), calls=%async_computation.1 | async-start | bytes 1572864 | tf_op jit(solution)/shard_map/all_to_all | solution.py:161
Sparse Core Ops, SparseCore 0:
  23.8 98.3 all-gather.2
  133.0 91.7 all-gather.4
